TPU v7x, 512 devices: a whole 4x4x16 slice. The times are simulated.
512 devices in a mesh: row: 32 (over x, z_lo, core), col: 16 (over z_hi, y).
Axes of the slice: x: 4, y: 4, z: 16 (z_hi: 4, z_lo: 4; z = z_hi * 4 + z_lo), core: 2. Of those that a mesh axis runs over, the one named last changes fastest.
Arguments:
- laplacian: bfloat16 [32768, 32768], P('row', 'col')
- interp: bfloat16 [32768, 128], P('row'), may hold values from -0.375 to 0.375
- vectors: bfloat16 [32, 32768], P(None, 'row'), may hold values from -6 to 6
- pairs: int32 [128, 2], replicated, may hold values from 0 to 255, as said below
Outputs:
- coarse: bfloat16 [16384, 16384], P(('row', 'col'))
- coarse_vectors: bfloat16 [32, 16384], P(None, 'row')
Inputs may be any that keep to these rules, and one draw needn't show every extreme that they name: Row c holds (a, b), where a lies among the 8 fine tile rows of row index g = (c // 4) mod 16, that is a // 8 == g, and b // 8 == g + 16. Every fine tile row appears exactly once in pairs.
All inputs are finite; a program needn't handle non-finite values.
Results may differ from a plain program's by a relative error of at most 0.0058.
Values may be sent and summed in bfloat16 or wider, within the bound.
A program may use at most 64 MiB of HBM per device.

v0:
```python
import jax
import jax.numpy as jnp
from jax import lax
from jax.sharding import PartitionSpec as P


def broadcast(array, axis, root):
    return lax.dynamic_index_in_dim(lax.all_gather(array, axis), root, 0, keepdims=False)


def from_partner(block, axis, bit):
    count = lax.axis_size(axis)
    route = []
    for low in range(count):
        high = low | 1 << bit
        if high != low and high < count:
            route += [(low, high), (high, low)]
    return lax.ppermute(block, axis, route)


def on_device(laplacian, interp, vectors, pairs):
    tile_size = interp.shape[1]
    fine_rows = interp.shape[0] // tile_size
    fine_cols = laplacian.shape[1] // tile_size
    vector_count = vectors.shape[0]
    row_count = lax.axis_size("row")
    col_count = lax.axis_size("col")
    row_ratio = row_count // col_count
    row_index = lax.axis_index("row")
    col_index = lax.axis_index("col")
    received = []
    for offset in range(row_ratio):
        received.append(broadcast(interp, "row", col_index * row_ratio + offset))
    col_interp = jnp.concatenate(received, axis=0)
    product = jnp.einsum(
        "xjy,jyb->xjb",
        laplacian.reshape(fine_rows * tile_size, fine_cols, tile_size),
        col_interp.reshape(fine_cols, tile_size, tile_size),
        preferred_element_type=jnp.float32,
    ).astype(jnp.bfloat16)
    row_blocks = interp.reshape(fine_rows, tile_size, tile_size)
    projected = jnp.einsum(
        "ixa,ixjb->iajb",
        row_blocks,
        product.reshape(fine_rows, tile_size, fine_cols, tile_size),
        preferred_element_type=jnp.float32,
    ).astype(jnp.bfloat16)
    projected = projected.reshape(fine_rows, tile_size, fine_cols * tile_size)
    restricted = jnp.einsum(
        "kix,ixa->kia",
        vectors.reshape(vector_count, fine_rows, tile_size),
        row_blocks,
        preferred_element_type=jnp.float32,
    ).astype(jnp.bfloat16)
    coarse_rows = fine_rows // 2
    upper_row = row_index >= row_count // 2
    partner_row = (row_index + row_count // 2) % row_count
    own_pairs = lax.dynamic_slice_in_dim(pairs, row_index * coarse_rows, coarse_rows, 0)
    local_rows = jnp.where(upper_row, own_pairs[:, 1], own_pairs[:, 0]) - row_index * fine_rows
    row_bit = row_count.bit_length() - 2
    mate_pairs = lax.dynamic_slice_in_dim(pairs, partner_row * coarse_rows, coarse_rows, 0)
    wanted = jnp.where(upper_row, mate_pairs[:, 1], mate_pairs[:, 0]) - row_index * fine_rows
    far_proj, far_vec = from_partner(
        (jnp.take(projected, wanted, axis=0), jnp.take(restricted, wanted, axis=1)), "row", row_bit
    )
    row_sum = jnp.take(projected, local_rows, axis=0).astype(jnp.float32) + far_proj.astype(
        jnp.float32
    )
    coarse_vectors = jnp.take(restricted, local_rows, axis=1).astype(jnp.float32) + far_vec.astype(
        jnp.float32
    )
    coarse_vectors = coarse_vectors.astype(jnp.bfloat16).reshape(
        vector_count, coarse_rows * tile_size
    )
    summed = row_sum.reshape(coarse_rows * tile_size, fine_cols, tile_size)
    strips = lax.all_to_all(
        summed.reshape(coarse_rows * tile_size, fine_cols * tile_size),
        "col",
        split_axis=0,
        concat_axis=1,
        tiled=True,
    )
    strip_rows = strips.shape[0]
    strips = strips.reshape(strip_rows, strips.shape[1] // tile_size, tile_size)
    low_member = pairs[:, 0]
    high_member = pairs[:, 1]
    coarse = (jnp.take(strips, low_member, axis=1) + jnp.take(strips, high_member, axis=1)).astype(
        jnp.bfloat16
    )
    coarse = coarse.reshape(strip_rows, pairs.shape[0] * tile_size)
    return (coarse, coarse_vectors)


def solution(mesh):
    placed = (P("row", "col"), P("row", None), P(None, "row"), P())
    return jax.shard_map(
        on_device,
        mesh=mesh,
        in_specs=placed,
        out_specs=(P(("row", "col"), None), P(None, "row")),
        check_vma=False,
    )
```

profile of v0, /device:TPU:96, one launch (start us, length us, event | category | flops | bytes accessed | tf_op | source)
XLA Modules:
  0.0 399.4 jit_solution(15776594169665902914)
XLA Ops:
  7.2 0.0 copy-start
  7.2 0.0 all-gather.3.cloned.1.call-start
  7.2 0.7 all-gather.3.cloned.1.call-update
  7.9 0.8 constant_dynamic-slice_fusion.1
  8.8 77.2 %all-gather.3.cloned.1.call-done = bf16[32768,128]{1,0:T(8,128)(2,1)} async-done(((bf16[1024,128]{1,0:T(8,128)(2,1)}), bf16[32768,128]{1,0:T(8,128)(2,1)}) %all-gather.3.cloned.1.call-update) | async-done | bytes 8388624 | tf_op jit(solution)/shard_map/all_gather | solution.py:8
  86.0 1.1 dynamic-slice_bitcast_fusion.1
  87.1 0.0 copy-start.1
  87.1 3.5 convert_bitcast_fusion
  90.7 3.2 fusion.8
  93.9 6.5 %copy.20 = bf16[8,128,2048]{2,1,0:T(8,128)(2,1)} copy(bf16[8,128,2048]{1,2,0:T(8,128)(2,1)} %bitcast.89) | data formatting | bytes 8388608 | tf_op jit(solution)/shard_map/reshape | solution.py:48
  100.4 2.9 gather_fusion.1
  103.3 1.6 broadcast_select_fusion
  104.9 3.9 collective-permute-start
  108.9 2.9 gather_fusion
  111.7 44.7 %collective-permute-done = bf16[4,128,2048]{2,1,0:T(8,128)(2,1)} collective-permute-done((bf16[4,128,2048]{2,1,0:T(8,128)(2,1)}, bf16[4,128,2048]{2,1,0:T(8,128)(2,1)}, u32[]{:S(2)}, u32[]{:S(2)}) %collective-permute-start) | collective-permute-done | bytes 2097184 | tf_op jit(solution)/shard_map/ppermute | solution.py:18
  156.4 4.5 %convert_add_fusion = f32[4,128,2048]{2,1,0:T(8,128)} fusion(bf16[4,128,2048]{2,1,0:T(8,128)(2,1)} %collective-permute-done, bf16[4,128,2048]{2,1,0:T(8,128)(2,1)S(1)} %gather_fusion, pred[4]{0:T(512)(128)(4,1)S(1)} %get-tuple-element.9), kind=kLoop, calls=%fused_computation.12 | loop fusion | flops 4194304 | bytes 8388612 | tf_op jit(solution)/shard_map/add | solution.py:66
  160.9 13.1 %all-to-all-start = ((f32[16,32,2048]{2,1,0:T(8,128)}), f32[16,32,2048]{2,1,0:T(8,128)}, u32[]{:S(2)}, u32[]{:S(2)}) async-start(f32[16,32,2048]{2,1,0:T(8,128)} %bitcast.88), calls=%async_computation | async-start | bytes 8388608 | tf_op jit(solution)/shard_map/all_to_all | solution.py:76
  174.0 0.0 copy-done
  174.0 0.2 fusion.12
  174.2 0.6 gather_fusion.5
  174.8 0.1 select_bitcast_fusion
  174.8 4.0 collective-permute-start.1
  178.8 0.6 gather_fusion.4
  179.4 2.7 collective-permute-done.1
  182.1 0.7 copy_bitcast_fusion.1
  182.8 181.9 %all-to-all-done = f32[16,32,2048]{2,1,0:T(8,128)} async-done(((f32[16,32,2048]{2,1,0:T(8,128)}), f32[16,32,2048]{2,1,0:T(8,128)}, u32[]{:S(2)}, u32[]{:S(2)}) %all-to-all-start) | async-done | bytes 4194336 | tf_op jit(solution)/shard_map/all_to_all | solution.py:76
  364.8 6.6 %copy.22 = f32[32,16,2048]{2,1,0:T(8,128)} copy(f32[32,16,2048]{2,0,1:T(8,128)} %bitcast.15) | data formatting | bytes 8388608 | tf_op jit(solution)/shard_map/all_to_all | solution.py:76
  371.3 4.9 %reshape.64 = f32[32,256,128]{2,1,0:T(8,128)} reshape(f32[32,16,2048]{2,1,0:T(8,128)} %copy.22) | data formatting | bytes 8388608 | tf_op jit(solution)/shard_map/reshape | solution.py:84
  376.2 6.6 %copy.23 = f32[32,256,128]{2,0,1:T(8,128)} copy(f32[32,256,128]{2,1,0:T(8,128)} %reshape.64) | data formatting | bytes 8388608 | tf_op jit(solution)/shard_map/reshape | solution.py:84
  382.8 2.9 gather_fusion.3
  385.7 4.2 %gather_fusion.2 = f32[128,32,128]{2,1,0:T(8,128)} fusion(f32[32,256,128]{2,0,1:T(8,128)} %copy.23, s32[1024]{0:T(1024)S(1)} %get-tuple-element.20), kind=kCustom, calls=%fused_computation.1.clone | custom fusion | bytes 4194816 | tf_op jit(solution)/shard_map/jit(_take)/gather | solution.py:87
  389.9 2.7 copy_bitcast_fusion
  (10 shorter events, 0.1 us)
Async XLA Ops:
  7.2 166.8 %copy-start = (bf16[32,1024]{1,0:T(8,128)(2,1)S(1)}, bf16[32,1024]{1,0:T(8,128)(2,1)}, u32[]{:S(2)}) copy-start(bf16[32,1024]{1,0:T(8,128)(2,1)} %param.12) | copy-start | bytes 196612
  7.2 78.8 %all-gather.3.cloned.1.call-start = ((), (), s32[]{:S(2)}) async-start(), calls=%async_computation.1 | async-start | bytes 8650752 | tf_op jit(solution)/shard_map/all_gather | solution.py:8
  87.1 3.6 copy-start.1
  104.9 51.5 %collective-permute-start = (bf16[4,128,2048]{2,1,0:T(8,128)(2,1)}, bf16[4,128,2048]{2,1,0:T(8,128)(2,1)}, u32[]{:S(2)}, u32[]{:S(2)}) collective-permute-start(bf16[4,128,2048]{2,1,0:T(8,128)(2,1)} %broadcast_select_fusion), channel_id=1, source_target_pairs={{0,256},{256,0},{16,272},{272,16},{32,288},{288,32},{48,304},{304,... | collective-permute-start | bytes 6291464 | tf_op jit(solution)/shard_map/ppermute | solution.py:18
  160.9 17.9 %copy-start.2 = (s32[128,2]{0,1:T(2,128)S(1)}, s32[128,2]{0,1:T(2,128)}, u32[]{:S(2)}) copy-start(s32[128,2]{0,1:T(2,128)} %param.13) | copy-start | bytes 3076
  160.9 203.9 %all-to-all-start = ((f32[16,32,2048]{2,1,0:T(8,128)}), f32[16,32,2048]{2,1,0:T(8,128)}, u32[]{:S(2)}, u32[]{:S(2)}) async-start(f32[16,32,2048]{2,1,0:T(8,128)} %bitcast.88), calls=%async_computation | async-start | bytes 8388608 | tf_op jit(solution)/shard_map/all_to_all | solution.py:76
  174.8 7.3 %collective-permute-start.1 = (bf16[32,4,128]{2,0,1:T(8,128)(2,1)S(1)}, bf16[32,4,128]{2,0,1:T(8,128)(2,1)S(1)}, u32[]{:S(2)}, u32[]{:S(2)}) collective-permute-start(bf16[32,4,128]{2,0,1:T(8,128)(2,1)S(1)} %select_bitcast_fusion), channel_id=1, source_target_pairs={{0,256},{256,0},{16,272},{272,16},{32,288},{288,32},{48,304},{304,... | collective-permute-start | bytes 98312 | tf_op jit(solution)/shard_map/ppermute | solution.py:18
Sparse Core Ops, SparseCore 0:
  10.1 75.8 all-gather.2
where the time goes:
time: 400 us; the launch traced here: 399 us
  waiting for transfers between devices  307 us (77%)
  local copies, waits for them, and re-layouts  40.4 us (10%)
  starting transfers between devices  21 us (5%)
  between operations  14.2 us (4%)
  other arithmetic  9.61 us (2%)
  matrix products  6.93 us (2%)
    all_to_all x1, waiting for transfers between devices, on_device(): lax.all_to_all(summed.reshape(coarse_rows * tile_size, fine_cols * tile_s...  182 us
    all_gather x1, waiting for transfers between devices, broadcast(): lax.all_gather(array, axis)  77.2 us
    ppermute x2, waiting for transfers between devices, from_partner(): return lax.ppermute(block, axis, route)  47.4 us
    all_to_all x1, starting transfers between devices, on_device(): lax.all_to_all(summed.reshape(coarse_rows * tile_size, fine_cols * tile_s...  13.1 us
    reshape x2, local copies, waits for them, and re-layouts, on_device(): strips = strips.reshape(strip_rows, strips.shape[1] // tile_size, tile_size)  11.5 us
  transfers between devices with their start and end apart: 4, of which 4 were waited for; matrix products, arithmetic and copies ran while one was open for 1% of the time, Pallas kernels for 0%

commit v1 on v0

v1 whole, which is shorter than its diff:
```python
import jax
import jax.numpy as jnp
from jax import lax
from jax.experimental import pallas as pl
from jax.experimental.pallas import tpu as pltpu
from jax.sharding import PartitionSpec as P

MESH = pl.DeviceIdType.MESH
F32 = jnp.float32
BF16 = jnp.bfloat16

TILE = 128
ROWS = 32
COLS = 16
FINE_ROWS = 8
FINE_COLS = 16
KEEP = 4
STEPS = 16
AHEAD = 6
FIRST = 1
WIDE = 4 * TILE
STRIP = 32
COARSE = 16384
PIECES = 4
HALF = PIECES // 2
PIECE = FINE_ROWS * TILE // PIECES


def prepare(
    pairs, lap_hbm, interp_hbm, vec_hbm, give_hbm, keep_hbm, block_hbm, vgive, vkeep,
    lap, own, vec, give, keep, block, in_sem, out_sem,
):
    row = lax.axis_index("row")
    col = lax.axis_index("col")
    partner = (row + ROWS // 2) % ROWS
    upper = row // (ROWS // 2)
    right = col // (COLS // 2)
    span = col % (COLS // 2)

    def wanted(k):
        return pairs[upper, KEEP * partner + k] - FINE_ROWS * row

    def kept(k):
        return pairs[upper, KEEP * row + k] - FINE_ROWS * row

    def tile_at(i):
        return pl.ds(pl.multiple_of(i * TILE, TILE), TILE)

    own_in = pltpu.make_async_copy(interp_hbm, own, in_sem.at[8])
    own_in.start()
    members = [wanted(k) for k in range(KEEP)] + [kept(k) for k in range(KEEP)]
    lap_in = []
    for n, i in enumerate(members):
        lap_in.append(pltpu.make_async_copy(lap_hbm.at[tile_at(i)], lap.at[n], in_sem.at[n]))
        lap_in[-1].start()
    vec_in = pltpu.make_async_copy(vec_hbm, vec, in_sem.at[9])
    vec_in.start()
    own_in.wait()

    for u in range(FINE_ROWS):
        d = (u // 4) * 64 + 4 * (row % (ROWS // 2)) + u % 4
        block[u * TILE : (u + 1) * TILE, :] = own[tile_at(pairs[upper, d] - FINE_ROWS * row), :]
    out = [pltpu.make_async_copy(block, block_hbm, out_sem.at[8])]
    out[0].start()

    vec_in.wait()
    for n, i in enumerate(members):
        part = jnp.dot(vec[:, tile_at(i)], own[tile_at(i), :], preferred_element_type=F32).astype(BF16)
        k = n % KEEP
        (vgive if n < KEEP else vkeep)[:, k * TILE : (k + 1) * TILE] = part

    across = [
        tile_at(pairs[right, (q % 2) * 64 + 8 * span + (q // 2) * 4 + v] - FINE_COLS * col)
        for q in range(4)
        for v in range(4)
    ]
    for n, i in enumerate(members):
        lap_in[n].wait()
        k = n % KEEP
        mine = own[tile_at(i), :]
        for q in range(4):
            wide = jnp.concatenate([lap[n, :, across[4 * q + v]] for v in range(4)], axis=1)
            part = lax.dot_general(mine, wide, (((0,), (0,)), ((), ())), preferred_element_type=F32)
            if n < KEEP:
                give[k, q] = part.astype(BF16)
            else:
                keep[k, q] = part
        src, dst = (give, give_hbm) if n < KEEP else (keep, keep_hbm)
        out.append(pltpu.make_async_copy(src.at[k], dst.at[k], out_sem.at[n]))
        out[-1].start()
    for copy in out:
        copy.wait()


def kernel(
    give, keep_hbm, block_hbm, vgive, vkeep, strips, cvec,
    keep, cols, trecv, rsend, vrecv,
    in_sem, xs_sem, xr_sem, zs_sem, zr_sem, ps_sem, pr_sem, v_sem, z_word, y_word,
):
    row = lax.axis_index("row")
    col = lax.axis_index("col")
    x, zlo, core = row // 8, (row // 2) % 4, row % 2
    zhi, y = col // 4, col % 4
    partner = (row + ROWS // 2) % ROWS
    x_up, x_down = (row + 8) % ROWS, (row + 24) % ROWS
    z_up, z_down = row + 2, row - 2
    twin = row + 1 - 2 * core

    barrier = pltpu.get_barrier_semaphore()

    def greet(r, c):
        pl.semaphore_signal(barrier, inc=1, device_id=(r, c), device_id_type=MESH)

    greet(partner, col)
    greet(x_up, col)
    greet(x_down, col)
    greet(twin, col)

    @pl.when(zlo < 3)
    def _():
        greet(z_up, col)

    @pl.when(zlo > 0)
    def _():
        greet(z_down, col)

    z_mates = [(zhi + 1) % 4 * 4 + y, (zhi + 3) % 4 * 4 + y]
    y_mates = [zhi * 4 + (y + o) % 4 for o in range(1, 4)]
    for c in z_mates + y_mates:
        greet(row, c)

    on_row = zlo == y
    dx = (x - zhi + 4) % 4
    is_source = jnp.logical_and(on_row, dx == 0)
    relay = jnp.logical_not(is_source)
    lead = core == 0
    follow = jnp.logical_not(lead)
    mine = pl.ds(pl.multiple_of(core * FINE_ROWS * TILE, FINE_ROWS * TILE), FINE_ROWS * TILE)

    @pl.when(is_source)
    def _():
        copy = pltpu.make_async_copy(block_hbm, cols.at[mine], in_sem.at[1])
        copy.start()
        copy.wait()

    keep_in = pltpu.make_async_copy(keep_hbm, keep, in_sem.at[0])
    keep_in.start()

    greeted = 9 + jnp.where(zlo < 3, 1, 0) + jnp.where(zlo > 0, 1, 0)
    pl.semaphore_wait(barrier, greeted)

    def piece_copy(p, f, target, sem):
        part = cols.at[pl.ds(pl.multiple_of(core * FINE_ROWS * TILE + p * PIECE, PIECE), PIECE)]
        return pltpu.make_async_remote_copy(
            src_ref=part, dst_ref=part, send_sem=ps_sem.at[p * 5 + f], recv_sem=pr_sem.at[sem],
            device_id=(target, col), device_id_type=MESH,
        )

    def forwards(p):
        first = dx == 1 if p % 2 == 0 else dx == 9
        second = dx == 3 if p % 2 == 1 else dx == 9
        return [
            (jnp.logical_and(on_row, jnp.logical_or(dx == 0, first)), piece_copy(p, 0, x_up, p)),
            (jnp.logical_and(on_row, jnp.logical_or(dx == 0, second)), piece_copy(p, 1, x_down, p)),
            (jnp.logical_and(zlo >= y, zlo < 3), piece_copy(p, 2, z_up, p)),
            (jnp.logical_and(zlo <= y, zlo > 0), piece_copy(p, 3, z_down, p)),
            (None, piece_copy(p, 4, twin, PIECES + p)),
        ]

    def when(test, act):
        if test is None:
            act()
        else:
            pl.when(test)(act)

    def pass_on(p):
        for test, copy in forwards(p):
            when(test, copy.start)

    def set_out():
        for p in range(PIECES):
            pass_on(p)

    def take_pieces():
        for p in range(PIECES):
            piece_copy(p, 0, twin, p).wait_recv()
            pass_on(p)

    def twin_half(n):
        for p in range(n * HALF, (n + 1) * HALF):
            other = cols.at[pl.ds(pl.multiple_of((1 - core) * FINE_ROWS * TILE + p * PIECE, PIECE), PIECE)]
            pltpu.make_async_remote_copy(
                src_ref=other, dst_ref=other, send_sem=ps_sem.at[p * 5 + 4], recv_sem=pr_sem.at[PIECES + p],
                device_id=(twin, col), device_id_type=MESH,
            ).wait_recv()

    def part_of(t):
        far = t < 12
        q = jnp.where(far, t // 3, t - 12)
        k = jnp.where(far, (zhi + t % 3 + 1) % 4, zhi)
        return k, q

    def x_copy(t):
        k, q = part_of(t)
        return pltpu.make_async_remote_copy(
            src_ref=give.at[k, q], dst_ref=trecv.at[t], send_sem=xs_sem.at[t], recv_sem=xr_sem.at[t],
            device_id=(partner, col), device_id_type=MESH,
        )

    pl.when(jnp.logical_and(lead, is_source))(set_out)
    for t in range(FIRST):
        x_copy(t).start()
    for c in z_mates:
        pl.semaphore_signal(z_word, inc=1, device_id=(row, c), device_id_type=MESH)
    pl.when(jnp.logical_and(lead, relay))(take_pieces)
    pl.semaphore_wait(z_word, 2)
    for c in y_mates:
        pl.semaphore_signal(y_word, inc=1, device_id=(row, c), device_id_type=MESH)
    pl.when(jnp.logical_and(follow, is_source))(set_out)
    pl.when(jnp.logical_and(follow, relay))(take_pieces)
    for t in range(FIRST, AHEAD):
        x_copy(t).start()
    v_copy = pltpu.make_async_remote_copy(
        src_ref=vgive, dst_ref=vrecv, send_sem=v_sem.at[0], recv_sem=v_sem.at[1],
        device_id=(partner, col), device_id_type=MESH,
    )
    v_copy.start()
    keep_in.wait()
    pl.semaphore_wait(y_word, 3)

    def window(c, q):
        start = (q % 2) * (COARSE // 2) + (2 * (c % 8) + q // 2) * WIDE
        return strips.at[c // 8, :, pl.ds(pl.multiple_of(start, WIDE), WIDE)]

    def quarter(t, at):
        return rsend.at[t, pl.ds(pl.multiple_of(at * STRIP, STRIP), STRIP)]

    def z_copy(t, o):
        k, q = part_of(t)
        at = (y + o) % 4
        return pltpu.make_async_remote_copy(
            src_ref=quarter(t, at), dst_ref=window(col, q), send_sem=zs_sem.at[t * 4 + o],
            recv_sem=zr_sem.at[col * 4 + q], device_id=(row, k * 4 + at), device_id_type=MESH,
        )

    def stay_copy(t):
        q = t - 12
        return pltpu.make_async_copy(quarter(t, y), window(col, q), zr_sem.at[col * 4 + q])

    def finish(t):
        @pl.when(t + AHEAD < STEPS)
        def _():
            x_copy(t + AHEAD).start()

        x_copy(t).wait_recv()
        k, q = part_of(t)
        total = (keep[k, q] + trecv[t].astype(F32)).astype(BF16)
        for v in range(4):
            here = slice(v * TILE, (v + 1) * TILE)
            there = pl.ds(pl.multiple_of((q * 4 + v) * TILE, TILE), TILE)
            rsend[t, :, here] = jnp.dot(
                total[:, here], cols[there, :], preferred_element_type=F32
            ).astype(BF16)

    def away(t, _):
        finish(t)
        for o in range(4):
            z_copy(t, o).start()
        return 0

    def near(t, _):
        finish(t)
        for o in range(1, 4):
            z_copy(t, o).start()
        stay_copy(t).start()
        return 0

    pl.when(follow)(lambda: twin_half(0))
    lax.fori_loop(0, 3, away, 0)
    pl.when(follow)(lambda: twin_half(1))
    lax.fori_loop(3, 6, away, 0)
    pl.when(lead)(lambda: twin_half(0))
    lax.fori_loop(6, 9, away, 0)
    pl.when(lead)(lambda: twin_half(1))
    lax.fori_loop(9, 12, away, 0)
    lax.fori_loop(12, STEPS, near, 0)

    v_copy.wait()
    cvec[...] = (vkeep[...].astype(F32) + vrecv[...].astype(F32)).astype(BF16)

    def drain(t, _):
        x_copy(t).wait_send()
        return 0

    lax.fori_loop(0, STEPS, drain, 0)

    def sent(t, _):
        for o in range(4):
            z_copy(t, o).wait_send()
        return 0

    def sent_near(t, _):
        for o in range(1, 4):
            z_copy(t, o).wait_send()
        stay_copy(t).wait()
        return 0

    lax.fori_loop(0, 12, sent, 0)
    lax.fori_loop(12, STEPS, sent_near, 0)
    for p in range(PIECES):
        for test, copy in forwards(p):
            when(test, copy.wait_send)

    def arrived(o, _):
        c = (col + o) % COLS
        for q in range(4):
            pltpu.make_async_remote_copy(
                src_ref=quarter(0, 0), dst_ref=window(c, q), send_sem=zs_sem.at[0],
                recv_sem=zr_sem.at[c * 4 + q], device_id=(row, c), device_id_type=MESH,
            ).wait_recv()
        return 0

    lax.fori_loop(1, COLS, arrived, 0)


def on_device(laplacian, interp, vectors, pairs):
    hbm = pl.BlockSpec(memory_space=pltpu.HBM)
    free = pl.BlockSpec(memory_space=pl.ANY)
    vmem = pl.BlockSpec(memory_space=pltpu.VMEM)
    dma = pltpu.SemaphoreType.DMA
    halves = (KEEP, 4, TILE, WIDE)
    block = (FINE_ROWS * TILE, TILE)
    side = (STRIP, KEEP * TILE)
    shape = jax.ShapeDtypeStruct
    give, keep, mine, vgive, vkeep = pl.pallas_call(
        prepare,
        out_shape=(shape(halves, BF16), shape(halves, F32), shape(block, BF16), shape(side, BF16), shape(side, BF16)),
        in_specs=[pl.BlockSpec(memory_space=pltpu.SMEM), hbm, hbm, hbm],
        out_specs=(free, free, free, vmem, vmem),
        scratch_shapes=[
            pltpu.VMEM((FINE_ROWS, TILE, FINE_COLS * TILE), BF16),
            pltpu.VMEM(block, BF16),
            pltpu.VMEM((STRIP, FINE_ROWS * TILE), BF16),
            pltpu.VMEM(halves, BF16),
            pltpu.VMEM(halves, F32),
            pltpu.VMEM(block, BF16),
            dma((10,)),
            dma((9,)),
        ],
        compiler_params=pltpu.CompilerParams(vmem_limit_bytes=62 * 1024 * 1024),
    )(pairs.T, laplacian, interp, vectors)
    strips, coarse_vectors = pl.pallas_call(
        kernel,
        out_shape=(shape((2, STRIP, COARSE), BF16), shape(side, BF16)),
        in_specs=[free, free, free, vmem, vmem],
        out_specs=(free, vmem),
        scratch_shapes=[
            pltpu.VMEM(halves, F32),
            pltpu.VMEM((FINE_COLS * TILE, TILE), BF16),
            pltpu.VMEM((STEPS, TILE, WIDE), BF16),
            pltpu.VMEM((STEPS, TILE, WIDE), BF16),
            pltpu.VMEM(side, BF16),
            dma((2,)),
            dma((STEPS,)),
            dma((STEPS,)),
            dma((4 * STEPS,)),
            dma((4 * COLS,)),
            dma((5 * PIECES,)),
            dma((2 * PIECES,)),
            dma((2,)),
            pltpu.SemaphoreType.REGULAR,
            pltpu.SemaphoreType.REGULAR,
        ],
        compiler_params=pltpu.CompilerParams(
            collective_id=0, has_side_effects=True, vmem_limit_bytes=62 * 1024 * 1024
        ),
    )(give, keep, mine, vgive, vkeep)
    coarse = (strips[0].astype(F32) + strips[1].astype(F32)).astype(BF16)
    return coarse, coarse_vectors


def solution(mesh):
    placed = (P("row", "col"), P("row", None), P(None, "row"), P())
    return jax.shard_map(
        on_device,
        mesh=mesh,
        in_specs=placed,
        out_specs=(P(("row", "col"), None), P(None, "row")),
        check_vma=False,
    )
```

time: 400 us -> 162 us (0.41)
  the two profiles are of different devices: /device:TPU:96 before, /device:TPU:66 now
where the time goes in v1:
time: 162 us; the launch traced here: 161 us
  Pallas kernels  157 us (97%)
  other arithmetic  2.75 us (2%)
    pallas_call x1, Pallas kernels, on_device(): pl.pallas_call(kernel, out_shape=(shape((2, STRIP, COARSE), BF16), shape(...  150 us
    pallas_call x1, Pallas kernels, on_device(): pl.pallas_call(prepare, out_shape=(shape(halves, BF16), shape(halves, F32...  7.56 us

profile of v1, /device:TPU:66, one launch (start us, length us, event | category | flops | bytes accessed | tf_op | source)
XLA Modules:
  0.0 161.3 jit_solution(10336066794380025914)
XLA Ops:
  0.6 7.6 %shard_map.59 = (bf16[4,4,128,512]{3,2,1,0:T(8,128)(2,1)}, f32[4,4,128,512]{3,2,1,0:T(8,128)}, bf16[1024,128]{1,0:T(8,128)(2,1)}, bf16[32,512]{1,0:T(8,128)(2,1)}, bf16[32,512]{1,0:T(8,128)(2,1)}) custom-call(s32[2,128]{1,0:T(2,128)} %bitcast.3, bf16[1024,2048]{1,0:T(8,128)(2,1)} %lap_hbm.1, bf16[1024,128]{1,0:T(8,128)(2,1)} %interp_hbm.1, ...), custom_call_target="tpu_custom_call" | custom-call | tf_op jit(solution)/shard_map/pallas_call | solution.py:335
  8.2 149.7 %shard_map.60 = (bf16[2,32,16384]{2,1,0:T(8,128)(2,1)}, bf16[32,512]{1,0:T(8,128)(2,1)}) custom-call(bf16[4,4,128,512]{3,2,1,0:T(8,128)(2,1)} %get-tuple-element.9.give, f32[4,4,128,512]{3,2,1,0:T(8,128)} %get-tuple-element.10.keep_hbm, bf16[1024,128]{1,0:T(8,128)(2,1)} %get-tuple-element.11.block_hbm, bf16[32,512]{1,0:T(8,128)(2,1)} %get-tuple-element.12.vgive, ...), custom_call_target="tpu_custom_call" | custom-call | tf_op jit(solution)/shard_map/pallas_call | solution.py:352
  157.9 0.0 copy-start
  157.9 2.8 %fusion = bf16[32,16384]{1,0:T(8,128)(2,1)} fusion(bf16[2,32,16384]{2,1,0:T(8,128)(2,1)} %get-tuple-element.14), kind=kLoop, calls=%fused_computation.1 | loop fusion | flops 2097152 | bytes 3145728 | tf_op jit(solution)/shard_map/convert_element_type | solution.py:378
  160.7 0.0 copy-done
  160.7 0.6 copy.7
Async XLA Ops:
  157.9 2.8 %copy-start = (bf16[32,512]{1,0:T(8,128)(2,1)S(1)}, bf16[32,512]{1,0:T(8,128)(2,1)}, u32[]{:S(2)}) copy-start(bf16[32,512]{1,0:T(8,128)(2,1)} %get-tuple-element.19) | copy-start | bytes 98308

commit v2 on v1

--- a/solution.py
+++ b/solution.py
@@ -16,8 +16,7 @@
 FINE_COLS = 16
 KEEP = 4
 STEPS = 16
-AHEAD = 6
-FIRST = 1
+AHEAD = 2
 WIDE = 4 * TILE
 STRIP = 32
 COARSE = 16384
@@ -103,7 +102,15 @@
     zhi, y = col // 4, col % 4
     partner = (row + ROWS // 2) % ROWS
     x_up, x_down = (row + 8) % ROWS, (row + 24) % ROWS
-    z_up, z_down = row + 2, row - 2
+    z = zhi * 4 + zlo
+
+    def along(d):
+        far = (z + d + 16) % 16
+        return x * 8 + far % 4 * 2 + core, far // 4 * 4 + y
+
+    line = [along(d) for d in (1, -1, 2, -2)]
+    served = [along(1), along(-1), along(2 - 4 * core)]
+    ring = [x_up, x_down, partner]
     twin = row + 1 - 2 * core
 
     barrier = pltpu.get_barrier_semaphore()
@@ -111,19 +118,10 @@
     def greet(r, c):
         pl.semaphore_signal(barrier, inc=1, device_id=(r, c), device_id_type=MESH)
 
-    greet(partner, col)
-    greet(x_up, col)
-    greet(x_down, col)
-    greet(twin, col)
-
-    @pl.when(zlo < 3)
-    def _():
-        greet(z_up, col)
-
-    @pl.when(zlo > 0)
-    def _():
-        greet(z_down, col)
-
+    for r in ring + [twin]:
+        greet(r, col)
+    for r, c in line:
+        greet(r, c)
     z_mates = [(zhi + 1) % 4 * 4 + y, (zhi + 3) % 4 * 4 + y]
     y_mates = [zhi * 4 + (y + o) % 4 for o in range(1, 4)]
     for c in z_mates + y_mates:
@@ -131,7 +129,9 @@
 
     on_row = zlo == y
     dx = (x - zhi + 4) % 4
-    is_source = jnp.logical_and(on_row, dx == 0)
+    column = dx == 0
+    aside = jnp.logical_not(column)
+    is_source = jnp.logical_and(on_row, column)
     relay = jnp.logical_not(is_source)
     lead = core == 0
     follow = jnp.logical_not(lead)
@@ -146,26 +146,30 @@
     keep_in = pltpu.make_async_copy(keep_hbm, keep, in_sem.at[0])
     keep_in.start()
 
-    greeted = 9 + jnp.where(zlo < 3, 1, 0) + jnp.where(zlo > 0, 1, 0)
-    pl.semaphore_wait(barrier, greeted)
+    pl.semaphore_wait(barrier, len(ring + line) + 1 + len(z_mates + y_mates))
+
+    def place(p):
+        return cols.at[pl.ds(pl.multiple_of(core * FINE_ROWS * TILE + p * PIECE, PIECE), PIECE)]
 
     def piece_copy(p, f, target, sem):
-        part = cols.at[pl.ds(pl.multiple_of(core * FINE_ROWS * TILE + p * PIECE, PIECE), PIECE)]
         return pltpu.make_async_remote_copy(
-            src_ref=part, dst_ref=part, send_sem=ps_sem.at[p * 5 + f], recv_sem=pr_sem.at[sem],
+            src_ref=place(p), dst_ref=place(p), send_sem=ps_sem.at[p * 7 + f], recv_sem=pr_sem.at[sem],
             device_id=(target, col), device_id_type=MESH,
         )
 
+    def serves(p):
+        out = []
+        for f, (r, c) in enumerate(served):
+            copy = pltpu.make_async_remote_copy(
+                src_ref=block_hbm.at[pl.ds(p * PIECE, PIECE)], dst_ref=place(p), send_sem=ps_sem.at[p * 7 + f],
+                recv_sem=pr_sem.at[p], device_id=(r, c), device_id_type=MESH,
+            )
+            out.append((jnp.logical_and(on_row, c // 4 == x), copy))
+        return out
+
     def forwards(p):
-        first = dx == 1 if p % 2 == 0 else dx == 9
-        second = dx == 3 if p % 2 == 1 else dx == 9
-        return [
-            (jnp.logical_and(on_row, jnp.logical_or(dx == 0, first)), piece_copy(p, 0, x_up, p)),
-            (jnp.logical_and(on_row, jnp.logical_or(dx == 0, second)), piece_copy(p, 1, x_down, p)),
-            (jnp.logical_and(zlo >= y, zlo < 3), piece_copy(p, 2, z_up, p)),
-            (jnp.logical_and(zlo <= y, zlo > 0), piece_copy(p, 3, z_down, p)),
-            (None, piece_copy(p, 4, twin, PIECES + p)),
-        ]
+        to_ring = [(column, piece_copy(p, 3 + f, r, p)) for f, r in enumerate(ring)]
+        return to_ring + [(None, piece_copy(p, 6, twin, PIECES + p))]
 
     def when(test, act):
         if test is None:
@@ -177,27 +181,31 @@
         for test, copy in forwards(p):
             when(test, copy.start)
 
-    def set_out():
+    def serve():
         for p in range(PIECES):
+            for test, copy in serves(p):
+                when(test, copy.start)
+
+    def take(low, high):
+        for p in range(low, high):
+            pl.when(relay)(piece_copy(p, 0, twin, p).wait_recv)
             pass_on(p)
 
-    def take_pieces():
-        for p in range(PIECES):
-            piece_copy(p, 0, twin, p).wait_recv()
-            pass_on(p)
+    def take_all():
+        take(0, PIECES)
 
     def twin_half(n):
         for p in range(n * HALF, (n + 1) * HALF):
             other = cols.at[pl.ds(pl.multiple_of((1 - core) * FINE_ROWS * TILE + p * PIECE, PIECE), PIECE)]
             pltpu.make_async_remote_copy(
-                src_ref=other, dst_ref=other, send_sem=ps_sem.at[p * 5 + 4], recv_sem=pr_sem.at[PIECES + p],
+                src_ref=other, dst_ref=other, send_sem=ps_sem.at[p * 7 + 6], recv_sem=pr_sem.at[PIECES + p],
                 device_id=(twin, col), device_id_type=MESH,
             ).wait_recv()
 
     def part_of(t):
         far = t < 12
         q = jnp.where(far, t // 3, t - 12)
-        k = jnp.where(far, (zhi + t % 3 + 1) % 4, zhi)
+        k = jnp.where(far, (zhi + 2 - t % 3 + t % 3 // 2 * 3) % 4, zhi)
         return k, q
 
     def x_copy(t):
@@ -207,18 +215,20 @@
             device_id=(partner, col), device_id_type=MESH,
         )
 
-    pl.when(jnp.logical_and(lead, is_source))(set_out)
-    for t in range(FIRST):
-        x_copy(t).start()
+    pl.when(lead)(serve)
+    pl.when(aside)(x_copy(0).start)
     for c in z_mates:
         pl.semaphore_signal(z_word, inc=1, device_id=(row, c), device_id_type=MESH)
-    pl.when(jnp.logical_and(lead, relay))(take_pieces)
+    pl.when(jnp.logical_and(lead, column))(take_all)
+    pl.when(column)(x_copy(0).start)
     pl.semaphore_wait(z_word, 2)
     for c in y_mates:
         pl.semaphore_signal(y_word, inc=1, device_id=(row, c), device_id_type=MESH)
-    pl.when(jnp.logical_and(follow, is_source))(set_out)
-    pl.when(jnp.logical_and(follow, relay))(take_pieces)
-    for t in range(FIRST, AHEAD):
+    pl.when(follow)(serve)
+    pl.when(jnp.logical_and(lead, aside))(lambda: take(0, HALF))
+    pl.when(jnp.logical_and(follow, column))(take_all)
+    pl.when(jnp.logical_and(follow, aside))(take_all)
+    for t in range(1, AHEAD):
         x_copy(t).start()
     v_copy = pltpu.make_async_remote_copy(
         src_ref=vgive, dst_ref=vrecv, send_sem=v_sem.at[0], recv_sem=v_sem.at[1],
@@ -277,6 +287,7 @@
 
     pl.when(follow)(lambda: twin_half(0))
     lax.fori_loop(0, 3, away, 0)
+    pl.when(jnp.logical_and(lead, aside))(lambda: take(HALF, PIECES))
     pl.when(follow)(lambda: twin_half(1))
     lax.fori_loop(3, 6, away, 0)
     pl.when(lead)(lambda: twin_half(0))
@@ -308,7 +319,7 @@
     lax.fori_loop(0, 12, sent, 0)
     lax.fori_loop(12, STEPS, sent_near, 0)
     for p in range(PIECES):
-        for test, copy in forwards(p):
+        for test, copy in serves(p) + forwards(p):
             when(test, copy.wait_send)
 
     def arrived(o, _):
@@ -365,7 +376,7 @@
             dma((STEPS,)),
             dma((4 * STEPS,)),
             dma((4 * COLS,)),
-            dma((5 * PIECES,)),
+            dma((7 * PIECES,)),
             dma((2 * PIECES,)),
             dma((2,)),
             pltpu.SemaphoreType.REGULAR,

time: 162 us -> 141 us (0.87)
  the two profiles are of different devices: /device:TPU:66 before, /device:TPU:1 now
where the time goes in v2:
time: 141 us
  Pallas kernels  137 us (97%)
  other arithmetic  2.75 us (2%)
    pallas_call x1, Pallas kernels, on_device(): pl.pallas_call(kernel, out_shape=(shape((2, STRIP, COARSE), BF16), shape(...  129 us
    pallas_call x1, Pallas kernels, on_device(): pl.pallas_call(prepare, out_shape=(shape(halves, BF16), shape(halves, F32...  7.55 us

profile of v2, /device:TPU:1, one launch (start us, length us, event | category | flops | bytes accessed | tf_op | source)
XLA Modules:
  0.0 141.0 jit_solution(7779791208104940722)
XLA Ops:
  0.6 7.6 %shard_map.59 = (bf16[4,4,128,512]{3,2,1,0:T(8,128)(2,1)}, f32[4,4,128,512]{3,2,1,0:T(8,128)}, bf16[1024,128]{1,0:T(8,128)(2,1)}, bf16[32,512]{1,0:T(8,128)(2,1)}, bf16[32,512]{1,0:T(8,128)(2,1)}) custom-call(s32[2,128]{1,0:T(2,128)} %bitcast.3, bf16[1024,2048]{1,0:T(8,128)(2,1)} %lap_hbm.1, bf16[1024,128]{1,0:T(8,128)(2,1)} %interp_hbm.1, ...), custom_call_target="tpu_custom_call" | custom-call | tf_op jit(solution)/shard_map/pallas_call | solution.py:346
  8.2 129.4 %shard_map.60 = (bf16[2,32,16384]{2,1,0:T(8,128)(2,1)}, bf16[32,512]{1,0:T(8,128)(2,1)}) custom-call(bf16[4,4,128,512]{3,2,1,0:T(8,128)(2,1)} %get-tuple-element.9.give, f32[4,4,128,512]{3,2,1,0:T(8,128)} %get-tuple-element.10.keep_hbm, bf16[1024,128]{1,0:T(8,128)(2,1)} %get-tuple-element.11.block_hbm, bf16[32,512]{1,0:T(8,128)(2,1)} %get-tuple-element.12.vgive, ...), custom_call_target="tpu_custom_call" | custom-call | tf_op jit(solution)/shard_map/pallas_call | solution.py:363
  137.6 0.0 copy-start
  137.6 2.8 %fusion = bf16[32,16384]{1,0:T(8,128)(2,1)} fusion(bf16[2,32,16384]{2,1,0:T(8,128)(2,1)} %get-tuple-element.14), kind=kLoop, calls=%fused_computation.1 | loop fusion | flops 2097152 | bytes 3145728 | tf_op jit(solution)/shard_map/convert_element_type | solution.py:389
  140.3 0.0 copy-done
  140.3 0.6 copy.7
Async XLA Ops:
  137.6 2.8 %copy-start = (bf16[32,512]{1,0:T(8,128)(2,1)S(1)}, bf16[32,512]{1,0:T(8,128)(2,1)}, u32[]{:S(2)}) copy-start(bf16[32,512]{1,0:T(8,128)(2,1)} %get-tuple-element.19) | copy-start | bytes 98308

commit v3 on v2

--- a/solution.py
+++ b/solution.py
@@ -20,7 +20,7 @@
 WIDE = 4 * TILE
 STRIP = 32
 COARSE = 16384
-PIECES = 4
+PIECES = 8
 HALF = PIECES // 2
 PIECE = FINE_ROWS * TILE // PIECES
 

time: 141 us -> 139 us (0.986)
  Pallas kernels: 137 us -> 134 us
    pallas_call x1, Pallas kernels: 129 us -> 127 us  [on_device(): pl.pallas_call(kernel, out_shape=(shape((2, STRIP, COARSE), BF16), shape(...]
where the time goes in v3:
time: 139 us; the launch traced here: 138 us
  Pallas kernels  134 us (96%)
  other arithmetic  2.75 us (2%)
    pallas_call x1, Pallas kernels, on_device(): pl.pallas_call(kernel, out_shape=(shape((2, STRIP, COARSE), BF16), shape(...  127 us
    pallas_call x1, Pallas kernels, on_device(): pl.pallas_call(prepare, out_shape=(shape(halves, BF16), shape(halves, F32...  7.55 us

profile of v3, /device:TPU:1, one launch (start us, length us, event | category | flops | bytes accessed | tf_op | source)
XLA Modules:
  0.0 138.3 jit_solution(18397912316797312492)
XLA Ops:
  0.6 7.5 %shard_map.59 = (bf16[4,4,128,512]{3,2,1,0:T(8,128)(2,1)}, f32[4,4,128,512]{3,2,1,0:T(8,128)}, bf16[1024,128]{1,0:T(8,128)(2,1)}, bf16[32,512]{1,0:T(8,128)(2,1)}, bf16[32,512]{1,0:T(8,128)(2,1)}) custom-call(s32[2,128]{1,0:T(2,128)} %bitcast.3, bf16[1024,2048]{1,0:T(8,128)(2,1)} %lap_hbm.1, bf16[1024,128]{1,0:T(8,128)(2,1)} %interp_hbm.1, ...), custom_call_target="tpu_custom_call" | custom-call | tf_op jit(solution)/shard_map/pallas_call | solution.py:346
  8.2 126.7 %shard_map.60 = (bf16[2,32,16384]{2,1,0:T(8,128)(2,1)}, bf16[32,512]{1,0:T(8,128)(2,1)}) custom-call(bf16[4,4,128,512]{3,2,1,0:T(8,128)(2,1)} %get-tuple-element.9.give, f32[4,4,128,512]{3,2,1,0:T(8,128)} %get-tuple-element.10.keep_hbm, bf16[1024,128]{1,0:T(8,128)(2,1)} %get-tuple-element.11.block_hbm, bf16[32,512]{1,0:T(8,128)(2,1)} %get-tuple-element.12.vgive, ...), custom_call_target="tpu_custom_call" | custom-call | tf_op jit(solution)/shard_map/pallas_call | solution.py:363
  134.9 0.0 copy-start
  134.9 2.8 %fusion = bf16[32,16384]{1,0:T(8,128)(2,1)} fusion(bf16[2,32,16384]{2,1,0:T(8,128)(2,1)} %get-tuple-element.14), kind=kLoop, calls=%fused_computation.1 | loop fusion | flops 2097152 | bytes 3145728 | tf_op jit(solution)/shard_map/convert_element_type | solution.py:389
  137.7 0.0 copy-done
  137.7 0.6 copy.7
Async XLA Ops:
  134.9 2.8 %copy-start = (bf16[32,512]{1,0:T(8,128)(2,1)S(1)}, bf16[32,512]{1,0:T(8,128)(2,1)}, u32[]{:S(2)}) copy-start(bf16[32,512]{1,0:T(8,128)(2,1)} %get-tuple-element.19) | copy-start | bytes 98308
